TPU v7x, 512 devices: a whole 4x4x16 slice. The times are simulated.
512 devices in a mesh: tgt: 16 (over y, x_lo, core), src: 32 (over z, x_hi).
Axes of the slice: x: 4 (x_hi: 2, x_lo: 2; x = x_hi * 2 + x_lo), y: 4, z: 16, core: 2. Of those that a mesh axis runs over, the one named last changes fastest.
Arguments:
- shear_leaves: bfloat16 [32, 32, 128, 128], P('tgt', 'src'), may hold values from -2 to 2, as said below
- normal_leaves: bfloat16 [32, 32, 128, 128], P('tgt', 'src'), may hold values from -2 to 2, as said below
- near_flags: int32 [32, 32], P('tgt', 'src'), may hold values from 0 to 1, as said below
- ranks: int32 [32, 32], P('tgt', 'src'), may hold values from 16 to 64
- shear_traction: float32 [4096, 128], P(('tgt', 'src')), may hold values from -1 to 1
- normal_traction: float32 [4096, 128], P(('tgt', 'src')), may hold values from 0.5 to 4
- state: float32 [4096, 128], P(('tgt', 'src')), may hold values from -0.5 to 0.5
- friction_a: float32 [4096, 128], P(('tgt', 'src')), may hold values from 1 to 2
- heal_rate: float32 [4096, 128], P(('tgt', 'src')), may hold values from 0.1 to 0.5
Outputs:
- shear_out: float32 [4096, 128], P(('tgt', 'src'))
- normal_out: float32 [4096, 128], P(('tgt', 'src'))
- state_out: float32 [4096, 128], P(('tgt', 'src'))
Inputs may be any that keep to these rules, and one draw needn't show every extreme that they name: `near_flags`: every leaf with equal leaf row and leaf column is 1, and a 1 stands only where the leaf row and the leaf column differ by at most 1. `shear_leaves`: columns 0 to 63 of an admissible leaf hold its factor U, columns 64 onward its factor V. `normal_leaves`: columns 0 to 63 of an admissible leaf hold its factor U, columns 64 onward its factor V.
All inputs are finite; a program needn't handle non-finite values.
Results may differ from a plain program's by a relative error of at most 0.002.
Values may be sent and summed in bfloat16 or wider, within the bound.
A program may use at most 64 MiB of HBM per device.

v0:
```python
import jax
import jax.numpy as jnp
from jax import lax
from jax.sharding import PartitionSpec as P

RMAX = 64
BLK = 128
time_step = 0.25


def spread(block, axis, owner):
    block = jnp.where(lax.axis_index(axis) == owner, block, jnp.zeros_like(block))
    return lax.psum(block, axis)


def kernel_terms(leaves, near_flags, ranks, source):
    leaf_rows, leaf_cols = near_flags.shape
    members = source.shape[-1]
    blocks = source.reshape(leaf_cols, BLK, members)
    factor_u = leaves[:, :, :, :RMAX]
    factor_v = leaves[:, :, :, RMAX:]
    inner = jnp.einsum("rcjk,cjn->rckn", factor_v, blocks, preferred_element_type=jnp.float32)
    keep_mask = (jnp.arange(RMAX, dtype=jnp.int32)[None, None, :] < ranks[:, :, None]) & (
        near_flags[:, :, None] == 0
    )
    inner = jnp.where(keep_mask[:, :, :, None], inner, 0.0).astype(jnp.bfloat16)
    lowrank = jnp.einsum("rcik,rckn->rin", factor_u, inner, preferred_element_type=jnp.float32)
    masked = jnp.where((near_flags == 1)[:, :, None, None], leaves, jnp.zeros((), leaves.dtype))
    dense_sum = jnp.einsum("rcij,cjn->rin", masked, blocks, preferred_element_type=jnp.float32)
    return (lowrank + dense_sum).reshape(leaf_rows * BLK, members)


def to_source(block_rows, leaf_rows, leaf_cols, src_index):
    first_leaf = src_index * leaf_cols
    offset = first_leaf % leaf_rows * BLK
    owner = first_leaf // leaf_rows
    piece = lax.dynamic_slice_in_dim(block_rows, offset, leaf_cols * BLK, 0)
    return spread(piece, "tgt", owner)


def friction(shear_now, normal_now, state_now, friction_a):
    effective = jnp.maximum(normal_now, 1.0)
    slip_rate = (
        2.0 * jnp.exp(-state_now / friction_a) * jnp.sinh(shear_now / (friction_a * effective))
    )
    return (slip_rate, (slip_rate - 1.0).astype(jnp.bfloat16))


def advance(rates, start):
    first_rates = rates(*start)
    first = tuple((value + time_step * change for value, change in zip(start, first_rates)))
    second_rates = rates(*first)
    second = tuple(
        (
            0.75 * begin + 0.25 * (value + time_step * change)
            for begin, value, change in zip(start, first, second_rates)
        )
    )
    third_rates = rates(*second)
    return tuple(
        (
            begin / 3.0 + 2.0 / 3.0 * (value + time_step * change)
            for begin, value, change in zip(start, second, third_rates)
        )
    )


def per_device(
    shear_leaves,
    normal_leaves,
    near_flags,
    ranks,
    shear_traction,
    normal_traction,
    state,
    friction_a,
    heal_rate,
):
    leaf_rows, leaf_cols = near_flags.shape
    src_index = lax.axis_index("src")

    def both_kernels(block_rows):
        source = to_source(block_rows, leaf_rows, leaf_cols, src_index)
        shear_part = kernel_terms(shear_leaves, near_flags, ranks, source)
        normal_part = kernel_terms(normal_leaves, near_flags, ranks, source)
        return (shear_part, normal_part)

    def own_rates(shear_now, normal_now, state_now):
        slip_rate, deviation = friction(shear_now, normal_now, state_now, friction_a)
        block_rows = lax.all_gather(deviation, "src", axis=0, tiled=True)
        shear_part, normal_part = both_kernels(block_rows)
        shear_rate, normal_rate = (
            lax.psum_scatter(shear_part, "src", scatter_dimension=0, tiled=True),
            lax.psum_scatter(normal_part, "src", scatter_dimension=0, tiled=True),
        )
        return (shear_rate, normal_rate, heal_rate * (jnp.exp(-state_now) - slip_rate))

    outputs = advance(own_rates, (shear_traction, normal_traction, state))
    return (outputs[0], outputs[1], outputs[2])


def solution(mesh):
    in_specs = (
        P("tgt", "src", None, None),
        P("tgt", "src", None, None),
        P("tgt", "src"),
        P("tgt", "src"),
        P(("tgt", "src"), None),
        P(("tgt", "src"), None),
        P(("tgt", "src"), None),
        P(("tgt", "src"), None),
        P(("tgt", "src"), None),
    )
    out_specs = (P(("tgt", "src"), None), P(("tgt", "src"), None), P(("tgt", "src"), None))
    return jax.shard_map(
        per_device, mesh=mesh, in_specs=in_specs, out_specs=out_specs, check_vma=False
    )
```

profile of v0, /device:TPU:8, one launch (start us, length us, event | category | flops | bytes accessed | tf_op | source)
XLA Modules:
  0.0 1324.7 jit_solution(18217465613332605597)
XLA Ops:
  7.3 0.6 copy-done.7
  8.0 82.7 %all_gather.9 = bf16[256,128]{1,0:T(8,128)(2,1)S(1)} all-gather(bf16[8,128]{1,0:T(8,128)(2,1)S(1)} %get-tuple-element.13), channel_id=1, replica_groups=mesh['tgt'=16,'src'=32] {'src'}, dimensions={0}, use_global_device_ids=true | all-gather | bytes 67584 | tf_op jit(solution)/shard_map/all_gather | solution.py:90
  90.7 46.2 %psum.21 = bf16[128,128]{1,0:T(8,128)(2,1)S(1)} all-reduce(bf16[128,128]{1,0:T(8,128)(2,1)S(1)} %dynamic-slice_select_fusion.2), channel_id=1, replica_groups=mesh['tgt'=16,'src'=32] {'tgt'}, use_global_device_ids=true, to_apply=%region_0.1 | all-reduce | flops 16384 | bytes 65536 | tf_op jit(solution)/shard_map/psum | solution.py:13
  137.0 0.7 copy-done
  138.8 0.7 copy-done.8
  139.5 0.9 fusion.1
  140.4 0.9 fusion
  141.3 1.3 dynamic-slice
  143.3 306.4 %all-reduce.17.cloned.1.call-done = (f32[256,128]{1,0:T(8,128)}, f32[256,128]{1,0:T(8,128)}) async-done(((f32[256,128]{1,0:T(8,128)}, f32[256,128]{1,0:T(8,128)}), (f32[256,128]{1,0:T(8,128)}, f32[256,128]{1,0:T(8,128)})) %all-reduce.17.cloned.1.call-update) | async-done | bytes 262160
  449.6 0.7 add_convert_fusion.1
  450.3 73.7 %all_gather.10 = bf16[256,128]{1,0:T(8,128)(2,1)S(1)} all-gather(bf16[8,128]{1,0:T(8,128)(2,1)S(1)} %get-tuple-element.11), channel_id=1, replica_groups=mesh['tgt'=16,'src'=32] {'src'}, dimensions={0}, use_global_device_ids=true | all-gather | bytes 67584 | tf_op jit(solution)/shard_map/all_gather | solution.py:90
  524.1 46.2 %psum.22 = bf16[128,128]{1,0:T(8,128)(2,1)S(1)} all-reduce(bf16[128,128]{1,0:T(8,128)(2,1)S(1)} %dynamic-slice_select_fusion.1), channel_id=1, replica_groups=mesh['tgt'=16,'src'=32] {'tgt'}, use_global_device_ids=true, to_apply=%region_3.4 | all-reduce | flops 16384 | bytes 65536 | tf_op jit(solution)/shard_map/psum | solution.py:13
  570.5 0.2 fusion.14
  570.9 0.9 fusion.3
  571.8 0.9 fusion.2
  572.8 310.1 %all-reduce.15.cloned.1.call-done = (f32[256,128]{1,0:T(8,128)}, f32[256,128]{1,0:T(8,128)}) async-done(((f32[256,128]{1,0:T(8,128)}, f32[256,128]{1,0:T(8,128)}), (f32[256,128]{1,0:T(8,128)}, f32[256,128]{1,0:T(8,128)})) %all-reduce.15.cloned.1.call-update) | async-done | bytes 262160
  882.9 1.3 multiply_add_fusion
  884.3 73.7 %all_gather.11 = bf16[256,128]{1,0:T(8,128)(2,1)S(1)} all-gather(bf16[8,128]{1,0:T(8,128)(2,1)S(1)} %add_convert_fusion), channel_id=1, replica_groups=mesh['tgt'=16,'src'=32] {'src'}, dimensions={0}, use_global_device_ids=true | all-gather | bytes 67584 | tf_op jit(solution)/shard_map/all_gather | solution.py:90
  958.0 46.2 %psum.23 = bf16[128,128]{1,0:T(8,128)(2,1)S(1)} all-reduce(bf16[128,128]{1,0:T(8,128)(2,1)S(1)} %dynamic-slice_select_fusion), channel_id=1, replica_groups=mesh['tgt'=16,'src'=32] {'tgt'}, use_global_device_ids=true, to_apply=%region_6.7 | all-reduce | flops 16384 | bytes 65536 | tf_op jit(solution)/shard_map/psum | solution.py:13
  1004.4 0.2 fusion.12
  1004.8 0.9 fusion.5
  1005.7 0.9 fusion.4
  1006.6 310.2 %all-reduce.13.cloned.1.call-done = (f32[256,128]{1,0:T(8,128)}, f32[256,128]{1,0:T(8,128)}) async-done(((f32[256,128]{1,0:T(8,128)}, f32[256,128]{1,0:T(8,128)}), (f32[256,128]{1,0:T(8,128)}, f32[256,128]{1,0:T(8,128)})) %all-reduce.13.cloned.1.call-update) | async-done | bytes 262160
  1316.8 1.4 fusion.71
  (42 shorter events, 2.4 us)
Async XLA Ops:
  7.2 442.5 %all-reduce.17.cloned.1.call-start = ((), (), s32[]{:S(2)}) async-start(), calls=%async_computation.2 | async-start | bytes 524288
  7.2 0.7 copy-start.5
  7.2 0.7 copy-start.4
  7.2 0.7 copy-start.7
  7.3 0.7 copy-start.3
  7.3 0.7 copy-start.2
  90.7 46.2 %copy-start.1 = (bf16[2,1,128,128]{3,2,1,0:T(8,128)(2,1)S(1)}, bf16[2,1,128,128]{3,2,1,0:T(8,128)(2,1)}, u32[]{:S(2)}) copy-start(bf16[2,1,128,128]{3,2,1,0:T(8,128)(2,1)} %param.9) | copy-start | bytes 196612
  136.9 0.8 copy-start
  138.8 0.7 copy-start.8
  141.3 741.6 %all-reduce.15.cloned.1.call-start = ((), (), s32[]{:S(2)}) async-start(), calls=%async_computation.1 | async-start | bytes 524288
  143.2 306.4 %copy-start.6 = (f32[8,128]{1,0:T(8,128)S(1)}, f32[8,128]{1,0:T(8,128)}, u32[]{:S(2)}) copy-start(f32[8,128]{1,0:T(8,128)} %param.17) | copy-start | bytes 12292
  572.7 744.1 %all-reduce.13.cloned.1.call-start = ((), (), s32[]{:S(2)}) async-start(), calls=%async_computation | async-start | bytes 524288
Sparse Core Ops, SparseCore 0:
  141.4 308.1 all-reduce.16
  572.8 310.0 all-reduce.14
  1006.7 310.0 all-reduce.12
where the time goes:
time: 1330 us; the launch traced here: 1320 us
  waiting for transfers between devices  927 us (70%)
  blocking collectives  369 us (28%)
  between operations  14.5 us (1%)
    unnamed x6, waiting for transfers between devices  927 us
    all_gather x3, blocking collectives, own_rates(): block_rows = lax.all_gather(deviation, 'src', axis=0, tiled=True)  230 us
    psum x3, blocking collectives, spread(): return lax.psum(block, axis)  139 us
  transfers between devices with their start and end apart: 3, of which 3 were waited for; matrix products, arithmetic and copies ran while one was open for 0% of the time, Pallas kernels for 0%

commit v1 on v0

--- a/solution.py
+++ b/solution.py
@@ -10,7 +10,7 @@
 
 def spread(block, axis, owner):
     block = jnp.where(lax.axis_index(axis) == owner, block, jnp.zeros_like(block))
-    return lax.psum(block, axis)
+    return jnp.sum(lax.all_gather(block, axis), axis=0)
 
 
 def kernel_terms(leaves, near_flags, ranks, source):

time: 1330 us -> 1230 us (0.925)
  blocking collectives: 369 us -> 285 us
    psum x3 -> x0, blocking collectives: 139 us -> none  [spread(): return lax.psum(block, axis)]
    all_gather x0 -> x3, blocking collectives: none -> 55.1 us  [spread(): return jnp.sum(lax.all_gather(block, axis), axis=0)]
where the time goes in v1:
time: 1230 us
  waiting for transfers between devices  917 us (75%)
  blocking collectives  285 us (23%)
  between operations  14.6 us (1%)
    unnamed x6, waiting for transfers between devices  917 us
    all_gather x3, blocking collectives, own_rates(): block_rows = lax.all_gather(deviation, 'src', axis=0, tiled=True)  230 us
    all_gather x3, blocking collectives, spread(): return jnp.sum(lax.all_gather(block, axis), axis=0)  55.1 us
  transfers between devices with their start and end apart: 3, of which 3 were waited for; matrix products, arithmetic and copies ran while one was open for 0% of the time, Pallas kernels for 0%

profile of v1, /device:TPU:8, one launch (start us, length us, event | category | flops | bytes accessed | tf_op | source)
XLA Modules:
  0.0 1231.6 jit_solution(3197148755778227197)
XLA Ops:
  7.3 0.6 copy-done.7
  8.0 82.7 %all_gather.27 = bf16[256,128]{1,0:T(8,128)(2,1)S(1)} all-gather(bf16[8,128]{1,0:T(8,128)(2,1)S(1)} %get-tuple-element.13), channel_id=1, replica_groups=mesh['tgt'=16,'src'=32] {'src'}, dimensions={0}, use_global_device_ids=true | all-gather | bytes 67584 | tf_op jit(solution)/shard_map/all_gather | solution.py:90
  90.8 0.7 copy-done
  91.7 18.5 %all-gather = bf16[2048,128]{1,0:T(8,128)(2,1)S(1)} all-gather(bf16[128,128]{1,0:T(8,128)(2,1)S(1)} %dynamic-slice_select_fusion.2), channel_id=2, replica_groups=mesh['tgt'=16,'src'=32] {'tgt'}, dimensions={0}, use_global_device_ids=true | all-gather | bytes 557056 | tf_op jit(solution)/shard_map/all_gather | solution.py:13
  111.2 0.7 copy-done.8
  111.9 0.9 fusion.1
  112.8 0.9 fusion
  113.7 1.3 dynamic-slice
  115.6 303.1 %all-reduce.17.cloned.1.call-done = (f32[256,128]{1,0:T(8,128)}, f32[256,128]{1,0:T(8,128)}) async-done(((f32[256,128]{1,0:T(8,128)}, f32[256,128]{1,0:T(8,128)}), (f32[256,128]{1,0:T(8,128)}, f32[256,128]{1,0:T(8,128)})) %all-reduce.17.cloned.1.call-update) | async-done | bytes 262160
  418.7 0.7 add_convert_fusion.1
  419.4 73.7 %all_gather.30 = bf16[256,128]{1,0:T(8,128)(2,1)S(1)} all-gather(bf16[8,128]{1,0:T(8,128)(2,1)S(1)} %get-tuple-element.11), channel_id=1, replica_groups=mesh['tgt'=16,'src'=32] {'src'}, dimensions={0}, use_global_device_ids=true | all-gather | bytes 67584 | tf_op jit(solution)/shard_map/all_gather | solution.py:90
  493.1 18.3 %all-gather.1 = bf16[2048,128]{1,0:T(8,128)(2,1)S(1)} all-gather(bf16[128,128]{1,0:T(8,128)(2,1)S(1)} %dynamic-slice_select_fusion.1), channel_id=3, replica_groups=mesh['tgt'=16,'src'=32] {'tgt'}, dimensions={0}, use_global_device_ids=true | all-gather | bytes 557056 | tf_op jit(solution)/shard_map/all_gather | solution.py:13
  511.8 0.2 fusion.14
  512.2 0.9 fusion.3
  513.1 0.9 fusion.2
  514.0 306.9 %all-reduce.15.cloned.1.call-done = (f32[256,128]{1,0:T(8,128)}, f32[256,128]{1,0:T(8,128)}) async-done(((f32[256,128]{1,0:T(8,128)}, f32[256,128]{1,0:T(8,128)}), (f32[256,128]{1,0:T(8,128)}, f32[256,128]{1,0:T(8,128)})) %all-reduce.15.cloned.1.call-update) | async-done | bytes 262160
  820.9 1.3 multiply_add_fusion
  822.3 73.7 %all_gather.33 = bf16[256,128]{1,0:T(8,128)(2,1)S(1)} all-gather(bf16[8,128]{1,0:T(8,128)(2,1)S(1)} %add_convert_fusion), channel_id=1, replica_groups=mesh['tgt'=16,'src'=32] {'src'}, dimensions={0}, use_global_device_ids=true | all-gather | bytes 67584 | tf_op jit(solution)/shard_map/all_gather | solution.py:90
  896.0 18.3 %all-gather.2 = bf16[2048,128]{1,0:T(8,128)(2,1)S(1)} all-gather(bf16[128,128]{1,0:T(8,128)(2,1)S(1)} %dynamic-slice_select_fusion), channel_id=4, replica_groups=mesh['tgt'=16,'src'=32] {'tgt'}, dimensions={0}, use_global_device_ids=true | all-gather | bytes 557056 | tf_op jit(solution)/shard_map/all_gather | solution.py:13
  914.6 0.2 fusion.12
  915.1 0.9 fusion.5
  915.9 0.9 fusion.4
  916.8 306.9 %all-reduce.13.cloned.1.call-done = (f32[256,128]{1,0:T(8,128)}, f32[256,128]{1,0:T(8,128)}) async-done(((f32[256,128]{1,0:T(8,128)}, f32[256,128]{1,0:T(8,128)}), (f32[256,128]{1,0:T(8,128)}, f32[256,128]{1,0:T(8,128)})) %all-reduce.13.cloned.1.call-update) | async-done | bytes 262160
  1223.7 1.4 fusion.71
  (45 shorter events, 2.7 us)
Async XLA Ops:
  7.2 411.5 %all-reduce.17.cloned.1.call-start = ((), (), s32[]{:S(2)}) async-start(), calls=%async_computation.2 | async-start | bytes 524288
  7.2 0.7 copy-start.7
  7.2 0.7 copy-start.2
  7.2 0.7 copy-start.3
  7.2 0.7 copy-start.4
  7.3 0.7 copy-start.5
  7.3 83.4 %copy-start.1 = (bf16[2,1,128,128]{3,2,1,0:T(8,128)(2,1)S(1)}, bf16[2,1,128,128]{3,2,1,0:T(8,128)(2,1)}, u32[]{:S(2)}) copy-start(bf16[2,1,128,128]{3,2,1,0:T(8,128)(2,1)} %param.9) | copy-start | bytes 196612
  90.7 0.8 copy-start
  111.2 0.7 copy-start.8
  113.7 707.3 %all-reduce.15.cloned.1.call-start = ((), (), s32[]{:S(2)}) async-start(), calls=%async_computation.1 | async-start | bytes 524288
  115.6 303.1 %copy-start.6 = (f32[8,128]{1,0:T(8,128)S(1)}, f32[8,128]{1,0:T(8,128)}, u32[]{:S(2)}) copy-start(f32[8,128]{1,0:T(8,128)} %param.17) | copy-start | bytes 12292
  514.0 709.7 %all-reduce.13.cloned.1.call-start = ((), (), s32[]{:S(2)}) async-start(), calls=%async_computation | async-start | bytes 524288
Sparse Core Ops, SparseCore 0:
  113.8 304.8 all-reduce.16
  514.1 306.7 all-reduce.14
  916.9 306.7 all-reduce.12

commit v2 on v0

--- a/solution.py
+++ b/solution.py
@@ -87,7 +87,9 @@
 
     def own_rates(shear_now, normal_now, state_now):
         slip_rate, deviation = friction(shear_now, normal_now, state_now, friction_a)
-        block_rows = lax.all_gather(deviation, "src", axis=0, tiled=True)
+        block_rows = jnp.concatenate(
+            lax.all_to_all(jnp.stack([deviation] * lax.axis_size("src")), "src", 0, 0), axis=0
+        )
         shear_part, normal_part = both_kernels(block_rows)
         shear_rate, normal_rate = (
             lax.psum_scatter(shear_part, "src", scatter_dimension=0, tiled=True),

time: 1330 us -> 1160 us (0.87)
  blocking collectives: 369 us -> 188 us
  starting transfers between devices: 0.12 us -> 18.2 us
    all_gather x3 -> x0, blocking collectives: 230 us -> none  [own_rates(): block_rows = lax.all_gather(deviation, 'src', axis=0, tiled=True)]
    all_to_all x0 -> x2, blocking collectives: none -> 48.8 us  [own_rates(): lax.all_to_all(jnp.stack([deviation] * lax.axis_size('src')), 'src', 0, 0)]
    all_to_all x0 -> x1, starting transfers between devices: none -> 18.1 us  [own_rates(): lax.all_to_all(jnp.stack([deviation] * lax.axis_size('src')), 'src', 0, 0)]
    unnamed x6, waiting for transfers between devices: 927 us -> 911 us
  transfers between devices with their start and end apart: 3 -> 4, of which waited for: 3 -> 4; matrix products, arithmetic and copies ran while one was open for 0% -> 0% of each run, Pallas kernels for 0% -> 0%
where the time goes in v2:
time: 1160 us
  waiting for transfers between devices  924 us (80%)
  blocking collectives  188 us (16%)
  starting transfers between devices  18.2 us (2%)
  between operations  14.6 us (1%)
    unnamed x6, waiting for transfers between devices  911 us
    psum x3, blocking collectives, spread(): return lax.psum(block, axis)  139 us
    all_to_all x2, blocking collectives, own_rates(): lax.all_to_all(jnp.stack([deviation] * lax.axis_size('src')), 'src', 0, 0)  48.8 us
  transfers between devices with their start and end apart: 4, of which 4 were waited for; matrix products, arithmetic and copies ran while one was open for 0% of the time, Pallas kernels for 0%

profile of v2, /device:TPU:8, one launch (start us, length us, event | category | flops | bytes accessed | tf_op | source)
XLA Modules:
  0.0 1160.7 jit_solution(11528724019531364798)
XLA Ops:
  7.2 0.8 add_convert_fusion.2
  7.9 0.6 stack.6
  8.6 18.1 %all-to-all-start = ((bf16[32,8,128]{2,1,0:T(8,128)(2,1)}), bf16[32,8,128]{2,1,0:T(8,128)(2,1)S(1)}, u32[]{:S(2)}, u32[]{:S(2)}) async-start(bf16[32,8,128]{2,1,0:T(8,128)(2,1)} %stack.6), calls=%async_computation | async-start | bytes 131072 | tf_op jit(solution)/shard_map/all_to_all | solution.py:91
  27.0 0.7 copy-done
  27.9 0.6 copy-done.8
  28.6 13.2 %all-to-all-done = bf16[32,8,128]{2,1,0:T(8,128)(2,1)S(1)} async-done(((bf16[32,8,128]{2,1,0:T(8,128)(2,1)}), bf16[32,8,128]{2,1,0:T(8,128)(2,1)S(1)}, u32[]{:S(2)}, u32[]{:S(2)}) %all-to-all-start) | async-done | bytes 65568 | tf_op jit(solution)/shard_map/all_to_all | solution.py:91
  41.9 47.1 %psum.21 = bf16[128,128]{1,0:T(8,128)(2,1)S(1)} all-reduce(bf16[128,128]{1,0:T(8,128)(2,1)S(1)} %dynamic-slice_select_fusion.2), channel_id=1, replica_groups=mesh['tgt'=16,'src'=32] {'tgt'}, use_global_device_ids=true, to_apply=%region_0.1 | all-reduce | flops 16384 | bytes 65536 | tf_op jit(solution)/shard_map/psum | solution.py:13
  89.6 0.9 fusion.1
  90.5 0.9 fusion
  91.5 1.3 dynamic-slice
  93.5 302.9 %all-reduce.17.cloned.1.call-done = (f32[256,128]{1,0:T(8,128)}, f32[256,128]{1,0:T(8,128)}) async-done(((f32[256,128]{1,0:T(8,128)}, f32[256,128]{1,0:T(8,128)}), (f32[256,128]{1,0:T(8,128)}, f32[256,128]{1,0:T(8,128)})) %all-reduce.17.cloned.1.call-update) | async-done | bytes 262160
  396.4 0.7 add_convert_fusion.1
  397.2 24.4 %all_to_all.15 = bf16[32,8,128]{2,1,0:T(8,128)(2,1)S(1)} all-to-all(bf16[32,8,128]{2,1,0:T(8,128)(2,1)S(1)} %stack.7), channel_id=1, replica_groups=mesh['tgt'=16,'src'=32] {'src'}, dimensions={0} | all-to-all | bytes 131072 | tf_op jit(solution)/shard_map/all_to_all | solution.py:91
  421.6 46.2 %psum.22 = bf16[128,128]{1,0:T(8,128)(2,1)S(1)} all-reduce(bf16[128,128]{1,0:T(8,128)(2,1)S(1)} %dynamic-slice_select_fusion.1), channel_id=1, replica_groups=mesh['tgt'=16,'src'=32] {'tgt'}, use_global_device_ids=true, to_apply=%region_3.4 | all-reduce | flops 16384 | bytes 65536 | tf_op jit(solution)/shard_map/psum | solution.py:13
  468.4 0.9 fusion.3
  469.3 0.9 fusion.2
  470.3 304.1 %all-reduce.15.cloned.1.call-done = (f32[256,128]{1,0:T(8,128)}, f32[256,128]{1,0:T(8,128)}) async-done(((f32[256,128]{1,0:T(8,128)}, f32[256,128]{1,0:T(8,128)}), (f32[256,128]{1,0:T(8,128)}, f32[256,128]{1,0:T(8,128)})) %all-reduce.15.cloned.1.call-update) | async-done | bytes 262160
  774.3 1.3 multiply_add_fusion
  775.7 24.4 %all_to_all.16 = bf16[32,8,128]{2,1,0:T(8,128)(2,1)S(1)} all-to-all(bf16[32,8,128]{2,1,0:T(8,128)(2,1)S(1)} %stack.8), channel_id=1, replica_groups=mesh['tgt'=16,'src'=32] {'src'}, dimensions={0} | all-to-all | bytes 131072 | tf_op jit(solution)/shard_map/all_to_all | solution.py:91
  800.1 46.2 %psum.23 = bf16[128,128]{1,0:T(8,128)(2,1)S(1)} all-reduce(bf16[128,128]{1,0:T(8,128)(2,1)S(1)} %dynamic-slice_select_fusion), channel_id=1, replica_groups=mesh['tgt'=16,'src'=32] {'tgt'}, use_global_device_ids=true, to_apply=%region_6.7 | all-reduce | flops 16384 | bytes 65536 | tf_op jit(solution)/shard_map/psum | solution.py:13
  847.0 0.9 fusion.5
  847.8 0.9 fusion.4
  848.8 304.1 %all-reduce.13.cloned.1.call-done = (f32[256,128]{1,0:T(8,128)}, f32[256,128]{1,0:T(8,128)}) async-done(((f32[256,128]{1,0:T(8,128)}, f32[256,128]{1,0:T(8,128)}), (f32[256,128]{1,0:T(8,128)}, f32[256,128]{1,0:T(8,128)})) %all-reduce.13.cloned.1.call-update) | async-done | bytes 262160
  1152.8 1.3 fusion.71
  (46 shorter events, 2.7 us)
Async XLA Ops:
  8.6 18.1 %copy-start.7 = (s32[2,1]{0,1:T(1,128)S(1)}, s32[2,1]{0,1:T(1,128)}, u32[]{:S(2)}) copy-start(s32[2,1]{0,1:T(1,128)} %param.11) | copy-start | bytes 28
  8.6 18.2 %copy-start.1 = (bf16[2,1,128,128]{3,2,1,0:T(8,128)(2,1)S(1)}, bf16[2,1,128,128]{3,2,1,0:T(8,128)(2,1)}, u32[]{:S(2)}) copy-start(bf16[2,1,128,128]{3,2,1,0:T(8,128)(2,1)} %param.9) | copy-start | bytes 196612
  8.6 33.3 %all-to-all-start = ((bf16[32,8,128]{2,1,0:T(8,128)(2,1)}), bf16[32,8,128]{2,1,0:T(8,128)(2,1)S(1)}, u32[]{:S(2)}, u32[]{:S(2)}) async-start(bf16[32,8,128]{2,1,0:T(8,128)(2,1)} %stack.6), calls=%async_computation | async-start | bytes 131072 | tf_op jit(solution)/shard_map/all_to_all | solution.py:91
  26.7 369.7 %all-reduce.17.cloned.1.call-start = ((), (), s32[]{:S(2)}) async-start(), calls=%async_computation.5 | async-start | bytes 524288
  26.8 0.8 copy-start
  27.9 0.7 copy-start.8
  91.4 305.0 %copy-start.5 = (f32[8,128]{1,0:T(8,128)S(1)}, f32[8,128]{1,0:T(8,128)}, u32[]{:S(2)}) copy-start(f32[8,128]{1,0:T(8,128)} %param.15) | copy-start | bytes 12292
  91.4 305.0 %copy-start.6 = (f32[8,128]{1,0:T(8,128)S(1)}, f32[8,128]{1,0:T(8,128)}, u32[]{:S(2)}) copy-start(f32[8,128]{1,0:T(8,128)} %param.17) | copy-start | bytes 12292
  91.4 682.9 %all-reduce.15.cloned.1.call-start = ((), (), s32[]{:S(2)}) async-start(), calls=%async_computation.4 | async-start | bytes 524288
  92.8 303.6 %copy-start.4 = (f32[8,128]{1,0:T(8,128)S(1)}, f32[8,128]{1,0:T(8,128)}, u32[]{:S(2)}) copy-start(f32[8,128]{1,0:T(8,128)} %param.16) | copy-start | bytes 12292
  92.8 303.6 %copy-start.3 = (f32[8,128]{1,0:T(8,128)S(1)}, f32[8,128]{1,0:T(8,128)}, u32[]{:S(2)}) copy-start(f32[8,128]{1,0:T(8,128)} %param.14) | copy-start | bytes 12292
  93.4 303.0 %copy-start.2 = (f32[8,128]{1,0:T(8,128)S(1)}, f32[8,128]{1,0:T(8,128)}, u32[]{:S(2)}) copy-start(f32[8,128]{1,0:T(8,128)} %param.13) | copy-start | bytes 12292
  470.2 682.6 %all-reduce.13.cloned.1.call-start = ((), (), s32[]{:S(2)}) async-start(), calls=%async_computation.3 | async-start | bytes 524288
Sparse Core Ops, SparseCore 0:
  91.6 304.7 all-reduce.16
  470.3 303.9 all-reduce.14
  848.9 303.9 all-reduce.12
